TPU v7x, 32 devices: a whole 2x2x4 slice. The times are simulated.
32 devices in a mesh: dp: 16 (over z, x, core), tensor: 2 (over y).
Axes of the slice: x: 2, y: 2, z: 4, core: 2. Of those that a mesh axis runs over, the one named last changes fastest.
Arguments:
- inputs: bfloat16 [16384, 1024], P(('dp', 'tensor')), may hold values from -6 to 6
- seg_ids: int32 [32, 512], P('dp'), may hold values from 0 to 15, never falling along the last dimension, each value on 1 to 384 neighbouring positions
- qkv_weight: float32 [2, 3, 1024, 1024], P(None, None, 'dp', 'tensor'), may hold values from -0.1875 to 0.1875
- out_weight: float32 [2, 1024, 1024], P(None, 'tensor', 'dp'), may hold values from -1.5 to 1.5
- up_weight: float32 [2, 1024, 4096], P(None, 'dp', 'tensor'), may hold values from -0.1875 to 0.1875
- down_weight: float32 [2, 4096, 1024], P(None, 'tensor', 'dp'), may hold values from -0.09375 to 0.09375
- norm_gains: float32 [2, 2, 1024], P(None, None, ('dp', 'tensor')), may hold values from 0.5 to 1.5
- row_biases: float32 [2, 6, 1024], P(None, None, ('dp', 'tensor')), may hold values from -2.5 to 2.5
- ff_bias: float32 [2, 4096], P(None, ('dp', 'tensor')), may hold values from -2.5 to 2.5
- cotangent: float32 [16384, 1024], P(('dp', 'tensor')), may hold values from -6 to 6
Outputs:
- outputs: bfloat16 [16384, 1024], P(('dp', 'tensor'))
- input_grad: float32 [16384, 1024], P(('dp', 'tensor'))
- qkv_grad: float32 [2, 3, 1024, 1024], P(None, None, 'dp', 'tensor')
- out_grad: float32 [2, 1024, 1024], P(None, 'tensor', 'dp')
- up_grad: float32 [2, 1024, 4096], P(None, 'dp', 'tensor')
- down_grad: float32 [2, 4096, 1024], P(None, 'tensor', 'dp')
- gains_grad: float32 [2, 2, 1024], P(None, None, ('dp', 'tensor'))
- biases_grad: float32 [2, 6, 1024], P(None, None, ('dp', 'tensor'))
- ff_bias_grad: float32 [2, 4096], P(None, ('dp', 'tensor'))
Inputs may be any that keep to these rules, and one draw needn't show every extreme that they name: `seg_ids`: within each sequence the document numbers never fall, and each document has 1 to 384 positions.
All inputs are finite; a program needn't handle non-finite values.
Results may differ from a plain program's by a relative error of at most 0.035.
Values may be sent and summed in bfloat16 or wider, within the bound.
No kernel may reach another device: no remote copies, remote signals or barrier semaphores. Data moves between devices by JAX's collectives and lax.ppermute only.
A program may use at most 256 MiB of HBM per device.

v0:
```python
from functools import partial
import jax
import jax.numpy as jnp
from jax import lax
from jax.sharding import PartitionSpec as P

HD = 64
EPSILON = 1e-06
HALF_ROOT = 0.7071067811865476
INV_ROOT_TAU = 0.3989422804014327


def normed(summed, gain_row, shift_row):
    centre = summed - jnp.mean(summed, axis=-1, keepdims=True)
    spread = jnp.mean(centre * centre, axis=-1, keepdims=True)
    return centre * lax.rsqrt(spread + EPSILON) * gain_row + shift_row


def gelu_slope(hidden_in):
    return (
        0.5 * (1.0 + lax.erf(hidden_in * HALF_ROOT))
        + hidden_in * jnp.exp(-0.5 * hidden_in * hidden_in) * INV_ROOT_TAU
    )


def collect(local_rows):
    return lax.all_gather(local_rows, "tensor", axis=0, tiled=True)


def reduce_rows(term_fn, row_count):
    return lax.psum_scatter(
        term_fn(jnp.int32(0), row_count * lax.axis_size("tensor")).astype(jnp.bfloat16),
        "tensor",
        scatter_dimension=0,
        tiled=True,
    ).astype(jnp.float32)


def project(operand, matrix, first_row, row_span):
    return jnp.dot(operand, matrix, preferred_element_type=jnp.float32)


def project_back(operand, matrix, first_row, row_span):
    return jnp.einsum("rf,df->rd", operand, matrix, preferred_element_type=jnp.float32)


def project_triple(operand, matrix, first_row, row_span):
    return jnp.einsum("rkc,kdc->rd", operand, matrix, preferred_element_type=jnp.float32)


def split_heads(matrix):
    return matrix.reshape(matrix.shape[0], matrix.shape[1] // HD, HD)


def masked_scores(query_heads, key_heads, segment):
    scores = jnp.einsum(
        "qhe,khe->hqk", query_heads, key_heads, preferred_element_type=jnp.float32
    ) * HD ** (-0.5)
    same_doc = segment[:, None] == segment[None, :]
    return jnp.where(same_doc[None], scores, -jnp.inf)


def attend_block(pieces):
    queries, key_rows, values, segment = pieces
    scores = masked_scores(split_heads(queries), split_heads(key_rows), segment)
    row_max = jnp.max(scores, axis=-1, keepdims=True)
    exp_scores = jnp.exp(scores - row_max)
    exp_total = jnp.sum(exp_scores, axis=-1, keepdims=True)
    attn_probs = (exp_scores / exp_total).astype(jnp.bfloat16)
    mixture = jnp.einsum(
        "hqk,khe->qhe", attn_probs, split_heads(values), preferred_element_type=jnp.float32
    )
    return (
        mixture.reshape(queries.shape).astype(jnp.bfloat16),
        (row_max + jnp.log(exp_total))[..., 0],
    )


def attend_back(pieces):
    queries, key_rows, values, segment, grad_mix, logsum = pieces
    query_heads = split_heads(queries)
    key_heads = split_heads(key_rows)
    value_heads = split_heads(values)
    grad_heads = split_heads(grad_mix)
    attn_probs = jnp.exp(masked_scores(query_heads, key_heads, segment) - logsum[..., None])
    grad_values = jnp.einsum(
        "hqk,qhe->khe",
        attn_probs.astype(jnp.bfloat16),
        grad_heads,
        preferred_element_type=jnp.float32,
    )
    grad_probs = jnp.einsum(
        "qhe,khe->hqk", grad_heads, value_heads, preferred_element_type=jnp.float32
    )
    inner_sum = jnp.sum(grad_probs * attn_probs, axis=-1, keepdims=True)
    grad_scores = (attn_probs * (grad_probs - inner_sum)).astype(jnp.bfloat16)
    grad_queries = jnp.einsum(
        "hqk,khe->qhe", grad_scores, key_heads, preferred_element_type=jnp.float32
    ) * HD ** (-0.5)
    grad_keys = jnp.einsum(
        "hqk,qhe->khe", grad_scores, query_heads, preferred_element_type=jnp.float32
    ) * HD ** (-0.5)
    stacked = jnp.stack([grad_queries, grad_keys, grad_values], axis=1)
    return stacked.reshape(queries.shape[0], 3, queries.shape[1]).astype(jnp.bfloat16)


def on_device(
    inputs,
    seg_ids,
    qkv_weight,
    out_weight,
    up_weight,
    down_weight,
    norm_gains,
    row_biases,
    ff_bias,
    cotangent,
):
    gain_rows, shift_rows, up_shifts = (
        lax.all_gather(norm_gains, ("dp", "tensor"), axis=2, tiled=True),
        lax.all_gather(row_biases, ("dp", "tensor"), axis=2, tiled=True),
        lax.all_gather(ff_bias, ("dp", "tensor"), axis=1, tiled=True),
    )
    tensor_rank = lax.axis_index("tensor")
    row_count = inputs.shape[0]
    model_width = inputs.shape[1]
    seq_count, length = seg_ids.shape
    head_cols = qkv_weight.shape[3]
    hidden = up_weight.shape[2]
    full_hidden = up_shifts.shape[1]
    layers = qkv_weight.shape[0]
    stream = inputs.astype(jnp.float32)
    stored = []
    for layer_index in range(layers):
        qkv_mat, out_mat, up_mat, down_mat = (
            lax.all_gather(qkv_weight[layer_index].astype(jnp.bfloat16), "dp", axis=1, tiled=True),
            lax.all_gather(out_weight[layer_index].astype(jnp.bfloat16), "dp", axis=1, tiled=True),
            lax.all_gather(up_weight[layer_index].astype(jnp.bfloat16), "dp", axis=0, tiled=True),
            lax.all_gather(down_weight[layer_index].astype(jnp.bfloat16), "dp", axis=1, tiled=True),
        )
        shifts = shift_rows[layer_index]
        query_shift = lax.dynamic_slice_in_dim(shifts[0], tensor_rank * head_cols, head_cols)
        value_shift = lax.dynamic_slice_in_dim(shifts[1], tensor_rank * head_cols, head_cols)
        up_shift = lax.dynamic_slice_in_dim(up_shifts[layer_index], tensor_rank * hidden, hidden)
        gathered = collect(stream.astype(jnp.bfloat16))
        projected = jnp.einsum("rd,kdc->rkc", gathered, qkv_mat, preferred_element_type=jnp.float32)
        projected = (
            projected + jnp.stack([query_shift, jnp.zeros_like(query_shift), value_shift])
        ).astype(jnp.bfloat16)
        by_sequence = projected.reshape(seq_count, length, 3, head_cols)
        mixture, logsum = lax.map(
            attend_block,
            (by_sequence[:, :, 0], by_sequence[:, :, 1], by_sequence[:, :, 2], seg_ids),
        )
        mixture = mixture.reshape(seq_count * length, head_cols)
        attended = reduce_rows(partial(project, mixture, out_mat), row_count)
        first_sum = stream + (attended + shifts[2])
        normed_mid = normed(first_sum, gain_rows[layer_index, 0], shifts[3])
        gathered_mid = collect(normed_mid.astype(jnp.bfloat16))
        hidden_in = jnp.dot(gathered_mid, up_mat, preferred_element_type=jnp.float32) + up_shift
        hidden_out = jax.nn.gelu(hidden_in, approximate=False).astype(jnp.bfloat16)
        branch_out = reduce_rows(partial(project, hidden_out, down_mat), row_count)
        second_sum = normed_mid + (branch_out + shifts[4])
        stream = normed(second_sum, gain_rows[layer_index, 1], shifts[5])
        stored.append(
            (
                qkv_mat,
                out_mat,
                up_mat,
                down_mat,
                gathered,
                projected,
                logsum,
                mixture,
                first_sum,
                gathered_mid,
                hidden_in,
                hidden_out,
                second_sum,
            )
        )
    grad_stream = cotangent
    weight_grads = [None] * layers
    small_grads = [None] * layers
    for layer_index in reversed(range(layers)):
        (
            qkv_mat,
            out_mat,
            up_mat,
            down_mat,
            gathered,
            projected,
            logsum,
            mixture,
            first_sum,
            gathered_mid,
            hidden_in,
            hidden_out,
            second_sum,
        ) = stored[layer_index]
        qkv_mat, out_mat, up_mat, down_mat = (
            lax.all_gather(qkv_weight[layer_index].astype(jnp.bfloat16), "dp", axis=1, tiled=True),
            lax.all_gather(out_weight[layer_index].astype(jnp.bfloat16), "dp", axis=1, tiled=True),
            lax.all_gather(up_weight[layer_index].astype(jnp.bfloat16), "dp", axis=0, tiled=True),
            lax.all_gather(down_weight[layer_index].astype(jnp.bfloat16), "dp", axis=1, tiled=True),
        )
        shifts = shift_rows[layer_index]
        layer_gains = gain_rows[layer_index]
        grad_second, grad_gain_late, grad_shift_late = jax.vjp(
            normed, second_sum, layer_gains[1], shifts[5]
        )[1](grad_stream)
        grad_branch = collect(grad_second.astype(jnp.bfloat16))
        grad_down = jnp.einsum(
            "rf,rd->fd", hidden_out, grad_branch, preferred_element_type=jnp.float32
        )
        grad_hidden = jnp.einsum(
            "rd,fd->rf", grad_branch, down_mat, preferred_element_type=jnp.float32
        )
        grad_pre = (grad_hidden * gelu_slope(hidden_in)).astype(jnp.bfloat16)
        grad_up = jnp.einsum(
            "rd,rf->df", gathered_mid, grad_pre, preferred_element_type=jnp.float32
        )
        grad_mid = grad_second + reduce_rows(partial(project_back, grad_pre, up_mat), row_count)
        grad_first, grad_gain_early, grad_shift_early = jax.vjp(
            normed, first_sum, layer_gains[0], shifts[3]
        )[1](grad_mid)
        grad_attn = collect(grad_first.astype(jnp.bfloat16))
        grad_out = jnp.einsum("rc,rd->cd", mixture, grad_attn, preferred_element_type=jnp.float32)
        grad_mix = jnp.einsum(
            "rd,cd->rc", grad_attn, out_mat, preferred_element_type=jnp.float32
        ).astype(jnp.bfloat16)
        by_sequence = projected.reshape(seq_count, length, 3, head_cols)
        grad_proj = lax.map(
            attend_back,
            (
                by_sequence[:, :, 0],
                by_sequence[:, :, 1],
                by_sequence[:, :, 2],
                seg_ids,
                grad_mix.reshape(seq_count, length, head_cols),
                logsum,
            ),
        )
        grad_proj = grad_proj.reshape(seq_count * length, 3, head_cols)
        grad_qkv = jnp.einsum(
            "rd,rkc->kdc", gathered, grad_proj, preferred_element_type=jnp.float32
        )
        grad_stream = grad_first + reduce_rows(
            partial(project_triple, grad_proj, qkv_mat), row_count
        )
        proj_sums = jnp.sum(grad_proj.astype(jnp.float32), axis=0)
        zero_row = jnp.zeros((model_width,), jnp.float32)
        grad_query_shift = lax.dynamic_update_slice_in_dim(
            zero_row, proj_sums[0], tensor_rank * head_cols, 0
        )
        grad_value_shift = lax.dynamic_update_slice_in_dim(
            zero_row, proj_sums[2], tensor_rank * head_cols, 0
        )
        grad_up_shift = lax.dynamic_update_slice_in_dim(
            jnp.zeros((full_hidden,), jnp.float32),
            jnp.sum(grad_pre.astype(jnp.float32), axis=0),
            tensor_rank * hidden,
            0,
        )
        small_grads[layer_index] = (
            jnp.stack([grad_gain_early, grad_gain_late]),
            jnp.stack(
                [
                    grad_query_shift,
                    grad_value_shift,
                    jnp.sum(grad_first, axis=0),
                    grad_shift_early,
                    jnp.sum(grad_second, axis=0),
                    grad_shift_late,
                ]
            ),
            grad_up_shift,
        )
        weight_grads[layer_index] = (
            lax.psum_scatter(
                grad_qkv.astype(jnp.bfloat16), "dp", scatter_dimension=1, tiled=True
            ).astype(jnp.float32),
            lax.psum_scatter(
                grad_out.astype(jnp.bfloat16), "dp", scatter_dimension=1, tiled=True
            ).astype(jnp.float32),
            lax.psum_scatter(
                grad_up.astype(jnp.bfloat16), "dp", scatter_dimension=0, tiled=True
            ).astype(jnp.float32),
            lax.psum_scatter(
                grad_down.astype(jnp.bfloat16), "dp", scatter_dimension=1, tiled=True
            ).astype(jnp.float32),
        )
    qkv_stack = jnp.stack([weight_grads[layer_index][0] for layer_index in range(layers)])
    out_stack = jnp.stack([weight_grads[layer_index][1] for layer_index in range(layers)])
    up_stack = jnp.stack([weight_grads[layer_index][2] for layer_index in range(layers)])
    down_stack = jnp.stack([weight_grads[layer_index][3] for layer_index in range(layers)])
    gains_all = jnp.stack([small_grads[layer_index][0] for layer_index in range(layers)])
    shifts_all = jnp.stack([small_grads[layer_index][1] for layer_index in range(layers)])
    hidden_all = jnp.stack([small_grads[layer_index][2] for layer_index in range(layers)])
    gains_grad, biases_grad, ff_bias_grad = (
        lax.psum_scatter(gains_all, ("dp", "tensor"), scatter_dimension=2, tiled=True),
        lax.psum_scatter(shifts_all, ("dp", "tensor"), scatter_dimension=2, tiled=True),
        lax.psum_scatter(hidden_all, ("dp", "tensor"), scatter_dimension=1, tiled=True),
    )
    return (
        stream.astype(jnp.bfloat16),
        grad_stream,
        qkv_stack,
        out_stack,
        up_stack,
        down_stack,
        gains_grad,
        biases_grad,
        ff_bias_grad,
    )


def solution(mesh):
    placed = (
        P(("dp", "tensor"), None),
        P("dp", None),
        P(None, None, "dp", "tensor"),
        P(None, "tensor", "dp"),
        P(None, "dp", "tensor"),
        P(None, "tensor", "dp"),
        P(None, None, ("dp", "tensor")),
        P(None, None, ("dp", "tensor")),
        P(None, ("dp", "tensor")),
        P(("dp", "tensor"), None),
    )
    return jax.shard_map(
        on_device,
        mesh=mesh,
        in_specs=placed,
        out_specs=(
            P(("dp", "tensor"), None),
            P(("dp", "tensor"), None),
            P(None, None, "dp", "tensor"),
            P(None, "tensor", "dp"),
            P(None, "dp", "tensor"),
            P(None, "tensor", "dp"),
            P(None, None, ("dp", "tensor")),
            P(None, None, ("dp", "tensor")),
            P(None, ("dp", "tensor")),
        ),
        check_vma=False,
    )
```

profile of v0, /device:TPU:0, one launch (start us, length us, event | category | flops | bytes accessed | tf_op | source)
XLA Modules:
  0.0 2121.0 jit_solution(10846130051365599466)
XLA Ops:
  12.5 79.0 %all_gather.67 = f32[2,6,1024]{1,0,2:T(2,128)S(1)} all-gather(f32[2,6,32]{1,0,2:T(2,128)S(1)} %copy.99), channel_id=1, replica_groups=mesh['dp'=16,'tensor'=2] {'dp','tensor'}, dimensions={2}, use_global_device_ids=true | all-gather | bytes 50688 | tf_op jit(solution)/shard_map/all_gather | solution.py:121
  91.5 27.6 %fusion.141 = (f32[1,1,1024]{1,0,2:T(1,128)S(1)}, f32[1,1,1024]{1,0,2:T(1,128)S(1)}, f32[1,1,1024]{1,0,2:T(1,128)S(1)}, f32[1024]{0:T(1024)S(1)}, f32[1024]{0:T(...) fusion(f32[2,6,1024]{1,0,2:T(2,128)S(1)} %all_gather.67), kind=kLoop, calls=%fused_computation.290 | loop fusion | bytes 98304 | tf_op jit(solution)/shard_map/slice | solution.py:142
  123.9 5.9 add_convert_fusion.1
  135.7 16.5 while.44
  153.1 4.2 convolution_convert_fusion.5
  158.6 72.7 %all_gather.69 = f32[2,2,1024]{1,0,2:T(2,128)S(1)} all-gather(f32[2,2,32]{1,0,2:T(2,128)S(1)} %copy.104), channel_id=1, replica_groups=mesh['dp'=16,'tensor'=2] {'dp','tensor'}, dimensions={2}, use_global_device_ids=true | all-gather | bytes 16896 | tf_op jit(solution)/shard_map/all_gather | solution.py:120
  231.3 26.9 %slice_reduce_fusion.1 = (f32[1024]{0:T(1024)}, f32[1024]{0:T(1024)}, f32[1024]{0:T(1024)S(1)}, f32[1024]{0:T(1024)S(1)}) fusion(f32[2,2,1024]{1,0,2:T(2,128)S(1)} %all_gather.69), kind=kLoop, calls=%fused_computation.222 | loop fusion | bytes 32768 | tf_op jit(solution)/shard_map/slice | solution.py:164
  264.5 65.2 %all_gather.72 = f32[2,4096]{1,0:T(2,128)S(1)} all-gather(f32[2,128]{1,0:T(2,128)S(1)} %copy-done.89), channel_id=1, replica_groups=mesh['dp'=16,'tensor'=2] {'dp','tensor'}, dimensions={1}, use_global_device_ids=true | all-gather | bytes 33792 | tf_op jit(solution)/shard_map/all_gather | solution.py:122
  330.3 25.8 %fusion.36 = (bf16[1024,2048]{1,0:T(8,128)(2,1)}, f32[1024,2048]{1,0:T(8,128)}) fusion(f32[2048]{0:T(1024)S(1)} %bitcast.432, bf16[1024,1024]{1,0:T(8,128)(2,1)} %all-gather.27.cloned.1.call-done, bf16[1,1024,2048]{2,1,0:T(8,128)(2,1)} %all-gather.45.cloned.1.call-done), kind=kOutput, calls=%fused_computation.80 | convolution fusion | flops 4433379328 | bytes 18882560 | tf_op jit(solution)/shard_map/dot_general | solution.py:160
  356.1 9.3 fusion.107
  366.3 27.6 %reduce-scatter.26.cloned.1.call-done = bf16[512,1024]{1,0:T(8,128)(2,1)} async-done(((bf16[1024,1024]{1,0:T(8,128)(2,1)}), bf16[512,1024]{1,0:T(8,128)(2,1)}) %reduce-scatter.26.cloned.1.call-update) | async-done | bytes 1048592 | tf_op jit(solution)/shard_map/reduce_scatter | solution.py:31
  399.8 41.4 %all-gather.49.cloned.1.call-done = bf16[1,3,1024,512]{3,2,1,0:T(8,128)(2,1)} async-done(((bf16[1,3,64,512]{3,2,1,0:T(8,128)(2,1)}), bf16[1,3,1024,512]{3,2,1,0:T(8,128)(2,1)}) %all-gather.49.cloned.1.call-update) | async-done | bytes 3145744 | tf_op jit(solution)/shard_map/all_gather | solution.py:136
  441.3 33.9 %all-gather.29.cloned.1.call-done = bf16[1024,1024]{1,0:T(8,128)(2,1)} async-done(((bf16[512,1024]{1,0:T(8,128)(2,1)}), bf16[1024,1024]{1,0:T(8,128)(2,1)}) %all-gather.29.cloned.1.call-update) | async-done | bytes 2097168 | tf_op jit(solution)/shard_map/all_gather | solution.py:27
  475.2 5.9 add_convert_fusion
  486.8 16.4 while.45
  503.3 12.0 all-gather.51.cloned.1.call-done
  515.3 4.1 convolution_convert_fusion.4
  520.3 30.1 %reduce-scatter.28.cloned.1.call-done = bf16[512,1024]{1,0:T(8,128)(2,1)} async-done(((bf16[1024,1024]{1,0:T(8,128)(2,1)}), bf16[512,1024]{1,0:T(8,128)(2,1)}) %reduce-scatter.28.cloned.1.call-update) | async-done | bytes 1048592 | tf_op jit(solution)/shard_map/reduce_scatter | solution.py:31
  556.0 48.1 %all-gather.53.cloned.1.call-done = bf16[1,1024,2048]{2,1,0:T(8,128)(2,1)} async-done(((bf16[1,64,2048]{2,1,0:T(8,128)(2,1)}), bf16[1,1024,2048]{2,1,0:T(8,128)(2,1)}) %all-gather.53.cloned.1.call-update) | async-done | bytes 4194320 | tf_op jit(solution)/shard_map/all_gather | solution.py:138
  604.1 33.7 %all-gather.31.cloned.1.call-done = bf16[1024,1024]{1,0:T(8,128)(2,1)} async-done(((bf16[512,1024]{1,0:T(8,128)(2,1)}), bf16[1024,1024]{1,0:T(8,128)(2,1)}) %all-gather.31.cloned.1.call-update) | async-done | bytes 2097168 | tf_op jit(solution)/shard_map/all_gather | solution.py:27
  637.8 25.6 %fusion.39 = (bf16[1024,2048]{1,0:T(8,128)(2,1)}, f32[1024,2048]{1,0:T(8,128)}) fusion(f32[2048]{0:T(1024)S(1)} %bitcast.435, bf16[1024,1024]{1,0:T(8,128)(2,1)} %all-gather.31.cloned.1.call-done, bf16[1,1024,2048]{2,1,0:T(8,128)(2,1)} %all-gather.53.cloned.1.call-done), kind=kOutput, calls=%fused_computation.83 | convolution fusion | flops 4433379328 | bytes 18882560 | tf_op jit(solution)/shard_map/dot_general | solution.py:160
  663.4 27.4 %all-gather.55.cloned.1.call-done = bf16[1,2048,1024]{1,2,0:T(8,128)(2,1)} async-done(((bf16[1,2048,64]{1,2,0:T(8,128)(2,1)}), bf16[1,2048,1024]{1,2,0:T(8,128)(2,1)}) %all-gather.55.cloned.1.call-update) | async-done | bytes 4194320 | tf_op jit(solution)/shard_map/all_gather | solution.py:139
  690.8 9.3 fusion.113
  700.2 30.4 %reduce-scatter.30.cloned.1.call-done = bf16[512,1024]{1,0:T(8,128)(2,1)} async-done(((bf16[1024,1024]{1,0:T(8,128)(2,1)}), bf16[512,1024]{1,0:T(8,128)(2,1)}) %reduce-scatter.30.cloned.1.call-update) | async-done | bytes 1048592 | tf_op jit(solution)/shard_map/reduce_scatter | solution.py:31
  739.1 33.0 %all-gather.33.cloned.1.call-done = bf16[1024,1024]{1,0:T(8,128)(2,1)} async-done(((bf16[512,1024]{1,0:T(8,128)(2,1)}), bf16[1024,1024]{1,0:T(8,128)(2,1)}) %all-gather.33.cloned.1.call-update) | async-done | bytes 2097168 | tf_op jit(solution)/shard_map/all_gather | solution.py:27
  772.1 11.4 convert_reduce_fusion
  785.5 5.7 fusion.110
  791.3 31.9 %reduce-scatter.32.cloned.1.call-done = bf16[512,1024]{1,0:T(8,128)(2,1)} async-done(((bf16[1024,1024]{1,0:T(8,128)(2,1)}), bf16[512,1024]{1,0:T(8,128)(2,1)}) %reduce-scatter.32.cloned.1.call-update) | async-done | bytes 1048592 | tf_op jit(solution)/shard_map/reduce_scatter | solution.py:31
  823.2 3.7 multiply_reduce_fusion.3
  830.7 33.0 %all-gather.35.cloned.1.call-done = bf16[1024,1024]{1,0:T(8,128)(2,1)} async-done(((bf16[512,1024]{1,0:T(8,128)(2,1)}), bf16[1024,1024]{1,0:T(8,128)(2,1)}) %all-gather.35.cloned.1.call-update) | async-done | bytes 2097168 | tf_op jit(solution)/shard_map/all_gather | solution.py:27
  863.6 3.8 convolution_convert_fusion.9
  869.4 32.0 %while.46 = (s32[]{:T(128)}, bf16[2,512,3,512]{1,3,2,0:T(8,128)(2,1)}, bf16[2,512,512]{1,2,0:T(8,128)(2,1)S(1)}, s32[2,512]{1,0:T(2,128)S(1)}, bf16[2,512,512]{1...) while((s32[]{:T(128)}, ...), condition=%wide.region_27.28_spmd, body=%wide.region_25.27_spmd.sunk | while | flops 1379921920 | bytes 102881448 | solution.py:233
  901.3 4.7 copy.110
  906.0 7.7 bitcast_convert_fusion.1
  914.3 31.5 %reduce-scatter.34.cloned.1.call-done = bf16[512,1024]{1,0:T(8,128)(2,1)} async-done(((bf16[1024,1024]{1,0:T(8,128)(2,1)}), bf16[512,1024]{1,0:T(8,128)(2,1)}) %reduce-scatter.34.cloned.1.call-update) | async-done | bytes 1048592 | tf_op jit(solution)/shard_map/reduce_scatter | solution.py:31
  953.0 33.2 %all-gather.37.cloned.1.call-done = bf16[1024,1024]{1,0:T(8,128)(2,1)} async-done(((bf16[512,1024]{1,0:T(8,128)(2,1)}), bf16[1024,1024]{1,0:T(8,128)(2,1)}) %all-gather.37.cloned.1.call-update) | async-done | bytes 2097168 | tf_op jit(solution)/shard_map/all_gather | solution.py:27
  986.3 10.8 convert_reduce_fusion.1
  999.1 5.7 fusion.104
  1004.9 31.9 %reduce-scatter.36.cloned.1.call-done = bf16[512,1024]{1,0:T(8,128)(2,1)} async-done(((bf16[1024,1024]{1,0:T(8,128)(2,1)}), bf16[512,1024]{1,0:T(8,128)(2,1)}) %reduce-scatter.36.cloned.1.call-update) | async-done | bytes 1048592 | tf_op jit(solution)/shard_map/reduce_scatter | solution.py:31
  1036.9 4.0 multiply_reduce_fusion.5
  1049.9 9.8 convolution_convert_fusion
  1061.3 8.3 convolution_convert_fusion.1
  1071.2 8.4 convolution_convert_fusion.2
  1082.1 9.4 convolution_convert_fusion.3
  1092.7 3.8 convolution_convert_fusion.8
  1098.5 32.0 %while.47 = (s32[]{:T(128)}, bf16[2,512,3,512]{1,3,2,0:T(8,128)(2,1)}, bf16[2,512,512]{1,2,0:T(8,128)(2,1)S(1)}, s32[2,512]{1,0:T(2,128)S(1)}, bf16[2,512,512]{1...) while((s32[]{:T(128)}, ...), condition=%wide.region_36.37_spmd, body=%wide.region_34.36_spmd.sunk | while | flops 1379921920 | bytes 102881448 | solution.py:233
  1135.1 3.9 convolution_convert_fusion.6
  1139.3 4.3 convolution_convert_fusion.7
  1143.8 6.5 convert_bitcast_fusion
  1150.3 7.8 copy.116
  1160.8 6.0 convert_bitcast_fusion.1
  1166.9 5.8 copy.114
  1174.6 6.5 bitcast_convert_fusion
  1182.4 35.2 %reduce-scatter.56.cloned.1.call-done = f32[128,2]{1,0:T(8,128)} async-done(((f32[4096,2]{1,0:T(8,128)}), f32[128,2]{1,0:T(8,128)}) %reduce-scatter.56.cloned.1.call-update) | async-done | bytes 1040
  1219.1 132.1 %reduce-scatter.52.cloned.1.call-done = f32[32,4]{1,0:T(8,128)} async-done(((f32[1024,4]{1,0:T(8,128)}), f32[32,4]{1,0:T(8,128)}) %reduce-scatter.52.cloned.1.call-update) | async-done | bytes 528
  1352.6 71.4 %reduce-scatter.50.cloned.1.call-done = bf16[2048,64]{0,1:T(8,128)(2,1)} async-done(((bf16[2048,1024]{0,1:T(8,128)(2,1)}), bf16[2048,64]{0,1:T(8,128)(2,1)}) %reduce-scatter.50.cloned.1.call-update) | async-done | bytes 262160 | tf_op jit(solution)/shard_map/reduce_scatter | solution.py:289
  1424.1 75.1 %reduce-scatter.48.cloned.1.call-done = bf16[2048,64]{0,1:T(8,128)(2,1)} async-done(((bf16[2048,1024]{0,1:T(8,128)(2,1)}), bf16[2048,64]{0,1:T(8,128)(2,1)}) %reduce-scatter.48.cloned.1.call-update) | async-done | bytes 262160 | tf_op jit(solution)/shard_map/reduce_scatter | solution.py:289
  1501.2 74.2 %reduce-scatter.46.cloned.1.call-done = bf16[64,2048]{1,0:T(8,128)(2,1)} async-done(((bf16[1024,2048]{1,0:T(8,128)(2,1)}), bf16[64,2048]{1,0:T(8,128)(2,1)}) %reduce-scatter.46.cloned.1.call-update) | async-done | bytes 262160 | tf_op jit(solution)/shard_map/reduce_scatter | solution.py:286
  1575.4 75.4 %reduce-scatter.44.cloned.1.call-done = bf16[64,2048]{1,0:T(8,128)(2,1)} async-done(((bf16[1024,2048]{1,0:T(8,128)(2,1)}), bf16[64,2048]{1,0:T(8,128)(2,1)}) %reduce-scatter.44.cloned.1.call-update) | async-done | bytes 262160 | tf_op jit(solution)/shard_map/reduce_scatter | solution.py:286
  1652.9 132.9 %reduce-scatter.54.cloned.1.call-done = f32[32,12]{1,0:T(8,128)} async-done(((f32[1024,12]{1,0:T(8,128)}), f32[32,12]{1,0:T(8,128)}) %reduce-scatter.54.cloned.1.call-update) | async-done | bytes 1552
  1787.2 55.5 %reduce-scatter.42.cloned.1.call-done = bf16[512,64]{0,1:T(8,128)(2,1)} async-done(((bf16[512,1024]{0,1:T(8,128)(2,1)}), bf16[512,64]{0,1:T(8,128)(2,1)}) %reduce-scatter.42.cloned.1.call-update) | async-done | bytes 65552 | tf_op jit(solution)/shard_map/reduce_scatter | solution.py:283
  1842.8 60.6 %reduce-scatter.40.cloned.1.call-done = bf16[512,64]{0,1:T(8,128)(2,1)} async-done(((bf16[512,1024]{0,1:T(8,128)(2,1)}), bf16[512,64]{0,1:T(8,128)(2,1)}) %reduce-scatter.40.cloned.1.call-update) | async-done | bytes 65552 | tf_op jit(solution)/shard_map/reduce_scatter | solution.py:283
  1905.0 171.3 %all-reduce.5.cloned.1.call-done = (bf16[3,1024,512]{2,0,1:T(4,128)(2,1)}, bf16[3,1024,512]{2,0,1:T(4,128)(2,1)}) async-done(((bf16[3,1024,512]{2,0,1:T(4,128)(2,1)}, bf16[3,1024,512]{2,0,1:T(4,128)(2,1)}), (bf16[3,1024,512]{2,0,1:T(4,128)(2,1)}, bf16[3,1024,512]{2,0,1:T(4,128)(2,1)})) %all-reduce.5.cloned.1.call-update) | async-done | bytes 6291472
  2079.9 31.1 %reduce-scatter.38.cloned.1.call-done = bf16[512,1024]{1,0:T(8,128)(2,1)} async-done(((bf16[1024,1024]{1,0:T(8,128)(2,1)}), bf16[512,1024]{1,0:T(8,128)(2,1)}) %reduce-scatter.38.cloned.1.call-update) | async-done | bytes 1048592 | tf_op jit(solution)/shard_map/reduce_scatter | solution.py:31
  (487 shorter events, 209.9 us)
Async XLA Ops:
  7.2 116.7 %all-gather.25.cloned.1.call-start = ((), (), s32[]{:S(2)}) async-start(), calls=%async_computation.17 | async-start | bytes 3145728 | tf_op jit(solution)/shard_map/all_gather | solution.py:27
  7.9 116.0 %all-gather.41.cloned.1.call-start = ((), (), s32[]{:S(2)}) async-start(), calls=%async_computation.39 | async-start | bytes 3342336 | tf_op jit(solution)/shard_map/all_gather | solution.py:136
  9.9 142.3 %all-gather.43.cloned.1.call-start = ((), (), s32[]{:S(2)}) async-start(), calls=%async_computation.40 | async-start | bytes 1114112 | tf_op jit(solution)/shard_map/all_gather | solution.py:137
  11.6 246.6 %reduce-scatter.24.cloned.1.call-start = ((), (), s32[]{:S(2)}) async-start(), calls=%async_computation.18 | async-start | bytes 3145728 | tf_op jit(solution)/shard_map/reduce_scatter | solution.py:31
  119.1 274.7 %copy-start.44 = (f32[1024]{0:T(1024)}, f32[1024]{0:T(1024)S(1)}, u32[]{:S(2)}) copy-start(f32[1024]{0:T(1024)S(1)} %get-tuple-element.406) | copy-start | bytes 12292
  157.4 100.8 %copy-start.2 = (bf16[512,1024]{1,0:T(8,128)(2,1)S(1)}, bf16[512,1024]{1,0:T(8,128)(2,1)}, u32[]{:S(2)}) copy-start(bf16[512,1024]{1,0:T(8,128)(2,1)} %param.18) | copy-start | bytes 3145732
  157.4 172.9 %all-gather.45.cloned.1.call-start = ((), (), s32[]{:S(2)}) async-start(), calls=%async_computation.41 | async-start | bytes 4456448 | tf_op jit(solution)/shard_map/all_gather | solution.py:138
  158.4 171.9 %all-gather.27.cloned.1.call-start = ((), (), s32[]{:S(2)}) async-start(), calls=%async_computation.19 | async-start | bytes 3145728 | tf_op jit(solution)/shard_map/all_gather | solution.py:27
  258.2 135.6 %copy-start.49 = (f32[1024]{0:T(1024)}, f32[1024]{0:T(1024)S(1)}, u32[]{:S(2)}) copy-start(f32[1024]{0:T(1024)S(1)} %get-tuple-element.293) | copy-start | bytes 12292
  258.2 292.2 %copy-start.46 = (f32[1024]{0:T(1024)}, f32[1024]{0:T(1024)S(1)}, u32[]{:S(2)}) copy-start(f32[1024]{0:T(1024)S(1)} %get-tuple-element.292) | copy-start | bytes 12292
  260.0 133.8 %copy-start.53 = (f32[512]{0:T(512)}, f32[512]{0:T(512)S(1)}, u32[]{:S(2)}) copy-start(f32[512]{0:T(512)S(1)} %broadcast_multiply_fusion.3) | copy-start | bytes 6148
  261.8 94.2 %copy-start.65 = (f32[512]{0:T(512)}, f32[512]{0:T(512)S(1)}, u32[]{:S(2)}) copy-start(f32[512]{0:T(512)S(1)} %multiply_reduce_fusion.13) | copy-start | bytes 6148
  261.8 132.0 %copy-start.57 = (f32[512]{0:T(512)}, f32[512]{0:T(512)S(1)}, u32[]{:S(2)}) copy-start(f32[512]{0:T(512)S(1)} %fusion.125) | copy-start | bytes 6148
  263.5 92.6 %all-gather.47.cloned.1.call-start = ((), (), s32[]{:S(2)}) async-start(), calls=%async_computation.42 | async-start | bytes 4456448 | tf_op jit(solution)/shard_map/all_gather | solution.py:139
  264.4 129.4 %reduce-scatter.26.cloned.1.call-start = ((), (), s32[]{:S(2)}) async-start(), calls=%async_computation.20 | async-start | bytes 3145728 | tf_op jit(solution)/shard_map/reduce_scatter | solution.py:31
  356.1 37.7 %copy-start.79 = (f32[1024]{0:T(1024)S(1)}, f32[1024]{0:T(1024)}, u32[]{:S(2)}) copy-start(f32[1024]{0:T(1024)} %get-tuple-element.408) | copy-start | bytes 12292
  365.5 75.8 %all-gather.49.cloned.1.call-start = ((), (), s32[]{:S(2)}) async-start(), calls=%async_computation.43 | async-start | bytes 3342336 | tf_op jit(solution)/shard_map/all_gather | solution.py:136
  366.2 109.0 %all-gather.29.cloned.1.call-start = ((), (), s32[]{:S(2)}) async-start(), calls=%async_computation.21 | async-start | bytes 3145728 | tf_op jit(solution)/shard_map/all_gather | solution.py:27
  396.1 79.1 %copy-start.84 = (f32[3,512]{1,0:T(4,128)S(1)}, f32[3,512]{1,0:T(4,128)}, u32[]{:S(2)}) copy-start(f32[3,512]{1,0:T(4,128)} %get-tuple-element.426) | copy-start | bytes 18436
  396.1 154.3 %copy-start.51 = (f32[512]{0:T(512)}, f32[512]{0:T(512)S(1)}, u32[]{:S(2)}) copy-start(f32[512]{0:T(512)S(1)} %broadcast_multiply_fusion.2) | copy-start | bytes 6148
  396.4 84.7 %copy-start.67 = (f32[512]{0:T(512)}, f32[512]{0:T(512)S(1)}, u32[]{:S(2)}) copy-start(f32[512]{0:T(512)S(1)} %multiply_reduce_fusion.12) | copy-start | bytes 6148
  396.5 154.0 %copy-start.55 = (f32[512]{0:T(512)}, f32[512]{0:T(512)S(1)}, u32[]{:S(2)}) copy-start(f32[512]{0:T(512)S(1)} %fusion.126) | copy-start | bytes 6148
  398.8 116.5 %all-gather.51.cloned.1.call-start = ((), (), s32[]{:S(2)}) async-start(), calls=%async_computation.44 | async-start | bytes 1114112 | tf_op jit(solution)/shard_map/all_gather | solution.py:137
  399.6 150.9 %reduce-scatter.28.cloned.1.call-start = ((), (), s32[]{:S(2)}) async-start(), calls=%async_computation.22 | async-start | bytes 3145728 | tf_op jit(solution)/shard_map/reduce_scatter | solution.py:31
  519.5 84.6 %all-gather.53.cloned.1.call-start = ((), (), s32[]{:S(2)}) async-start(), calls=%async_computation.45 | async-start | bytes 4456448 | tf_op jit(solution)/shard_map/all_gather | solution.py:138
  520.3 117.5 %all-gather.31.cloned.1.call-start = ((), (), s32[]{:S(2)}) async-start(), calls=%async_computation.23 | async-start | bytes 3145728 | tf_op jit(solution)/shard_map/all_gather | solution.py:27
  553.5 110.0 %copy-start.69 = (f32[512]{0:T(512)}, f32[512]{0:T(512)S(1)}, u32[]{:S(2)}) copy-start(f32[512]{0:T(512)S(1)} %multiply_reduce_fusion.11) | copy-start | bytes 6148
  554.9 135.9 %all-gather.55.cloned.1.call-start = ((), (), s32[]{:S(2)}) async-start(), calls=%async_computation.46 | async-start | bytes 4456448 | tf_op jit(solution)/shard_map/all_gather | solution.py:139
  555.5 175.1 %reduce-scatter.30.cloned.1.call-start = ((), (), s32[]{:S(2)}) async-start(), calls=%async_computation.24 | async-start | bytes 3145728 | tf_op jit(solution)/shard_map/reduce_scatter | solution.py:31
  690.8 39.8 %copy-start.72 = (f32[1024]{0:T(1024)S(1)}, f32[1024]{0:T(1024)}, u32[]{:S(2)}) copy-start(f32[1024]{0:T(1024)} %get-tuple-element.412) | copy-start | bytes 12292
  700.2 72.0 %all-gather.33.cloned.1.call-start = ((), (), s32[]{:S(2)}) async-start(), calls=%async_computation.25 | async-start | bytes 3145728 | tf_op jit(solution)/shard_map/all_gather | solution.py:27
  738.9 84.3 %reduce-scatter.32.cloned.1.call-start = ((), (), s32[]{:S(2)}) async-start(), calls=%async_computation.26 | async-start | bytes 3145728 | tf_op jit(solution)/shard_map/reduce_scatter | solution.py:31
  791.2 72.4 %all-gather.35.cloned.1.call-start = ((), (), s32[]{:S(2)}) async-start(), calls=%async_computation.27 | async-start | bytes 3145728 | tf_op jit(solution)/shard_map/all_gather | solution.py:27
  830.4 115.4 %reduce-scatter.34.cloned.1.call-start = ((), (), s32[]{:S(2)}) async-start(), calls=%async_computation.28 | async-start | bytes 3145728 | tf_op jit(solution)/shard_map/reduce_scatter | solution.py:31
  830.6 38.8 %copy-start.7 = (bf16[2,512,512]{1,2,0:T(8,128)(2,1)S(1)}, bf16[2,512,512]{1,2,0:T(8,128)(2,1)}, u32[]{:S(2)}) copy-start(bf16[2,512,512]{1,2,0:T(8,128)(2,1)} %copy-done.6) | copy-start | bytes 3145732
  830.6 38.8 %copy-start.11 = (bf16[2,512,512]{1,2,0:T(8,128)(2,1)S(1)}, bf16[2,512,512]{1,2,0:T(8,128)(2,1)}, u32[]{:S(2)}) copy-start(bf16[2,512,512]{1,2,0:T(8,128)(2,1)} %copy-done.10) | copy-start | bytes 3145732
  830.6 38.7 %copy-start.39 = (s32[2,512]{1,0:T(2,128)S(1)}, s32[2,512]{1,0:T(2,128)}, u32[]{:S(2)}) copy-start(s32[2,512]{1,0:T(2,128)} %copy-done.38) | copy-start | bytes 12292
  830.7 38.7 %copy-start.43 = (f32[2,8,512]{2,1,0:T(8,128)S(1)}, f32[2,8,512]{2,1,0:T(8,128)}, u32[]{:S(2)}) copy-start(f32[2,8,512]{2,1,0:T(8,128)} %copy-done.42) | copy-start | bytes 98308
  906.0 39.8 %copy-start.1 = (f32[512,1024]{1,0:T(8,128)S(1)}, f32[512,1024]{1,0:T(8,128)}, u32[]{:S(2)}) copy-start(f32[512,1024]{1,0:T(8,128)} %copy-done) | copy-start | bytes 6291460
  906.0 39.8 %copy-start.47 = (f32[1024]{0:T(1024)S(1)}, f32[1024]{0:T(1024)}, u32[]{:S(2)}) copy-start(f32[1024]{0:T(1024)} %copy-done.46) | copy-start | bytes 12292
  906.0 39.8 %copy-start.52 = (f32[512]{0:T(512)S(1)}, f32[512]{0:T(512)}, u32[]{:S(2)}) copy-start(f32[512]{0:T(512)} %copy-done.51) | copy-start | bytes 6148
  906.0 39.8 %copy-start.56 = (f32[512]{0:T(512)S(1)}, f32[512]{0:T(512)}, u32[]{:S(2)}) copy-start(f32[512]{0:T(512)} %copy-done.55) | copy-start | bytes 6148
  913.8 72.5 %all-gather.37.cloned.1.call-start = ((), (), s32[]{:S(2)}) async-start(), calls=%async_computation.29 | async-start | bytes 3145728 | tf_op jit(solution)/shard_map/all_gather | solution.py:27
  953.0 83.8 %reduce-scatter.36.cloned.1.call-start = ((), (), s32[]{:S(2)}) async-start(), calls=%async_computation.30 | async-start | bytes 3145728 | tf_op jit(solution)/shard_map/reduce_scatter | solution.py:31
  999.0 37.8 %copy-start.3 = (bf16[512,1024]{1,0:T(8,128)(2,1)S(1)}, bf16[512,1024]{1,0:T(8,128)(2,1)}, u32[]{:S(2)}) copy-start(bf16[512,1024]{1,0:T(8,128)(2,1)} %param.18) | copy-start | bytes 3145732
  999.0 37.8 %copy-start.13 = (bf16[512,1024]{1,0:T(8,128)(2,1)S(1)}, bf16[512,1024]{1,0:T(8,128)(2,1)}, u32[]{:S(2)}) copy-start(bf16[512,1024]{1,0:T(8,128)(2,1)} %reduce-scatter.24.cloned.1.call-done) | copy-start | bytes 3145732
  999.1 37.8 %copy-start.45 = (f32[1024]{0:T(1024)S(1)}, f32[1024]{0:T(1024)}, u32[]{:S(2)}) copy-start(f32[1024]{0:T(1024)} %copy-done.44) | copy-start | bytes 12292
  999.1 37.8 %copy-start.50 = (f32[1024]{0:T(1024)S(1)}, f32[1024]{0:T(1024)}, u32[]{:S(2)}) copy-start(f32[1024]{0:T(1024)} %copy-done.49) | copy-start | bytes 12292
  999.1 37.8 %copy-start.54 = (f32[512]{0:T(512)S(1)}, f32[512]{0:T(512)}, u32[]{:S(2)}) copy-start(f32[512]{0:T(512)} %copy-done.53) | copy-start | bytes 6148
  999.1 37.8 %copy-start.58 = (f32[512]{0:T(512)S(1)}, f32[512]{0:T(512)}, u32[]{:S(2)}) copy-start(f32[512]{0:T(512)} %copy-done.57) | copy-start | bytes 6148
  1004.8 86.9 %all-gather.39.cloned.1.call-start = ((), (), s32[]{:S(2)}) async-start(), calls=%async_computation.31 | async-start | bytes 3145728 | tf_op jit(solution)/shard_map/all_gather | solution.py:27
  1045.3 172.3 %reduce-scatter.56.cloned.1.call-start = ((), (), s32[]{:S(2)}) async-start(), calls=%async_computation.49 | async-start | bytes 2162688
  1047.6 303.6 %reduce-scatter.52.cloned.1.call-start = ((), (), s32[]{:S(2)}) async-start(), calls=%async_computation.47 | async-start | bytes 540672
  1049.7 374.4 %reduce-scatter.50.cloned.1.call-start = ((), (), s32[]{:S(2)}) async-start(), calls=%async_computation.38 | async-start | bytes 4456448 | tf_op jit(solution)/shard_map/reduce_scatter | solution.py:289
  1059.8 439.4 %reduce-scatter.48.cloned.1.call-start = ((), (), s32[]{:S(2)}) async-start(), calls=%async_computation.37 | async-start | bytes 4456448 | tf_op jit(solution)/shard_map/reduce_scatter | solution.py:289
  1069.6 505.8 %reduce-scatter.46.cloned.1.call-start = ((), (), s32[]{:S(2)}) async-start(), calls=%async_computation.36 | async-start | bytes 4456448 | tf_op jit(solution)/shard_map/reduce_scatter | solution.py:286
  1079.6 571.2 %reduce-scatter.44.cloned.1.call-start = ((), (), s32[]{:S(2)}) async-start(), calls=%async_computation.35 | async-start | bytes 4456448 | tf_op jit(solution)/shard_map/reduce_scatter | solution.py:286
  1091.5 694.2 %reduce-scatter.54.cloned.1.call-start = ((), (), s32[]{:S(2)}) async-start(), calls=%async_computation.48 | async-start | bytes 540672
  1135.1 707.7 %reduce-scatter.42.cloned.1.call-start = ((), (), s32[]{:S(2)}) async-start(), calls=%async_computation.34 | async-start | bytes 1114112 | tf_op jit(solution)/shard_map/reduce_scatter | solution.py:283
  1139.0 764.3 %reduce-scatter.40.cloned.1.call-start = ((), (), s32[]{:S(2)}) async-start(), calls=%async_computation.33 | async-start | bytes 1114112 | tf_op jit(solution)/shard_map/reduce_scatter | solution.py:283
  1143.7 932.6 %all-reduce.5.cloned.1.call-start = ((), (), s32[]{:S(2)}) async-start(), calls=%async_computation.50 | async-start | bytes 16777216
  1172.7 938.2 %reduce-scatter.38.cloned.1.call-start = ((), (), s32[]{:S(2)}) async-start(), calls=%async_computation.32 | async-start | bytes 3145728 | tf_op jit(solution)/shard_map/reduce_scatter | solution.py:31
  1181.1 929.8 %copy-start.27 = (f32[512,1024]{1,0:T(8,128)S(1)}, f32[512,1024]{1,0:T(8,128)}, u32[]{:S(2)}) copy-start(f32[512,1024]{1,0:T(8,128)} %copy-done.26) | copy-start | bytes 6291460
  1181.1 929.8 %copy-start.64 = (f32[512]{0:T(512)S(1)}, f32[512]{0:T(512)}, u32[]{:S(2)}) copy-start(f32[512]{0:T(512)} %copy-done.63) | copy-start | bytes 6148
  (73 other events, 773.6 us)
Sparse Core Ops, SparseCore 0:
  9.6 44.2 all-gather.24
  56.6 47.1 all-gather.40
  106.6 36.7 all-gather.42
  157.5 37.1 reduce-scatter.23
  197.5 50.7 all-gather.44
  263.6 30.7 all-gather.26
  297.3 50.5 all-gather.46
  365.6 28.1 reduce-scatter.25
  396.0 45.1 all-gather.48
  443.2 31.9 all-gather.28
  477.4 37.9 all-gather.50
  519.6 30.7 reduce-scatter.27
  553.4 50.6 all-gather.52
  606.2 31.6 all-gather.30
  640.1 50.7 all-gather.54
  700.3 30.3 reduce-scatter.29
  739.0 33.0 all-gather.32
  791.3 31.8 reduce-scatter.31
  830.5 33.1 all-gather.34
  913.9 31.8 reduce-scatter.33
  953.1 33.1 all-gather.36
  1005.0 31.8 reduce-scatter.35
  1045.5 33.1 all-gather.38
  1080.8 136.7 reduce-scatter.55
  1220.4 130.7 reduce-scatter.51
  1355.4 68.6 reduce-scatter.49
  1427.8 71.3 reduce-scatter.47
  1503.5 71.8 reduce-scatter.45
  1579.3 71.4 reduce-scatter.43
  1653.0 132.7 reduce-scatter.53
  1789.4 53.3 reduce-scatter.41
  1846.8 56.5 reduce-scatter.39
  1907.0 169.2 all-reduce.4
  2079.2 31.6 reduce-scatter.37
where the time goes:
time: 2130 us; the launch traced here: 2120 us
  waiting for transfers between devices  1400 us (66%)
  matrix products  253 us (12%)
  blocking collectives  217 us (10%)
  local copies, waits for them, and re-layouts  158 us (7%)
  other arithmetic  73.7 us (3%)
    unnamed x38, waiting for transfers between devices  475 us
    reduce_scatter x8, waiting for transfers between devices, reduce_rows(): lax.psum_scatter(term_fn(jnp.int32(0), row_count * lax.axis_size('tensor'...  214 us
    all_gather x8, waiting for transfers between devices, collect(): return lax.all_gather(local_rows, 'tensor', axis=0, tiled=True)  167 us
    reduce_scatter x2, waiting for transfers between devices, on_device(): lax.psum_scatter(grad_up.astype(jnp.bfloat16), 'dp', scatter_dimension=0,...  150 us
    reduce_scatter x2, waiting for transfers between devices, on_device(): lax.psum_scatter(grad_down.astype(jnp.bfloat16), 'dp', scatter_dimension=...  147 us
    reduce_scatter x2, waiting for transfers between devices, on_device(): lax.psum_scatter(grad_out.astype(jnp.bfloat16), 'dp', scatter_dimension=1...  116 us
    all_gather x1, blocking collectives, on_device(): lax.all_gather(row_biases, ('dp', 'tensor'), axis=2, tiled=True)  79 us
    all_gather x1, blocking collectives, on_device(): lax.all_gather(norm_gains, ('dp', 'tensor'), axis=2, tiled=True)  72.7 us
  transfers between devices with their start and end apart: 34, of which 26 were waited for; matrix products, arithmetic and copies ran while one was open for 15% of the time, Pallas kernels for 0%

commit v1 on v0

--- a/solution.py
+++ b/solution.py
@@ -8,6 +8,37 @@
 EPSILON = 1e-06
 HALF_ROOT = 0.7071067811865476
 INV_ROOT_TAU = 0.3989422804014327
+
+
+def order_regions(vec, row_dim):
+    comm_axis = "dp"
+    x_now, tile_out, vec_out = (
+        lax.axis_size(comm_axis),
+        lax.axis_index(comm_axis),
+        vec.shape[row_dim],
+    )
+    res = lax.dynamic_update_slice_in_dim(
+        jnp.zeros(
+            [idx * x_now if kk == row_dim else idx for kk, idx in enumerate(vec.shape)], vec.dtype
+        ),
+        vec,
+        tile_out * vec_out,
+        axis=row_dim,
+    )
+    a_now = heard = vec
+    j = 1
+    while j < x_now // 2 + 1:
+        a_now = lax.ppermute(a_now, comm_axis, [(kk, (kk + 1) % x_now) for kk in range(x_now)])
+        res = lax.dynamic_update_slice_in_dim(
+            res, a_now, (tile_out - j) % x_now * vec_out, axis=row_dim
+        )
+        if 2 * j < x_now:
+            heard = lax.ppermute(heard, comm_axis, [(kk, (kk - 1) % x_now) for kk in range(x_now)])
+            res = lax.dynamic_update_slice_in_dim(
+                res, heard, (tile_out + j) % x_now * vec_out, axis=row_dim
+            )
+        j = j + 1
+    return res
 
 
 def normed(summed, gain_row, shift_row):
@@ -135,7 +166,7 @@
         qkv_mat, out_mat, up_mat, down_mat = (
             lax.all_gather(qkv_weight[layer_index].astype(jnp.bfloat16), "dp", axis=1, tiled=True),
             lax.all_gather(out_weight[layer_index].astype(jnp.bfloat16), "dp", axis=1, tiled=True),
-            lax.all_gather(up_weight[layer_index].astype(jnp.bfloat16), "dp", axis=0, tiled=True),
+            order_regions(up_weight[layer_index].astype(jnp.bfloat16), 0),
             lax.all_gather(down_weight[layer_index].astype(jnp.bfloat16), "dp", axis=1, tiled=True),
         )
         shifts = shift_rows[layer_index]

time: 2130 us -> 2260 us (1.061)
  starting transfers between devices: 3.5 us -> 65.8 us
  matrix products: 253 us -> 282 us
    ppermute x0 -> x30, starting transfers between devices: none -> 62.4 us  [the longest x14 62.1 us: order_regions(): lax.ppermute(heard, comm_axis, [(kk, (kk - 1) % x_now) for kk in range(x_...]
    ppermute x0 -> x30, waiting for transfers between devices: none -> 58.8 us  [the longest x16 58 us: order_regions(): lax.ppermute(a_now, comm_axis, [(kk, (kk + 1) % x_now) for kk in range(x_...]
    all_gather x8, waiting for transfers between devices: 167 us -> 132 us  [collect(): return lax.all_gather(local_rows, 'tensor', axis=0, tiled=True)]
    all_gather x2, waiting for transfers between devices: 48.1 us -> 81.7 us  [on_device(): lax.all_gather(up_weight[layer_index].astype(jnp.bfloat16), 'dp', axis=0,...]
    all_gather x2, waiting for transfers between devices: 27.4 us -> 0.01 us  [on_device(): lax.all_gather(down_weight[layer_index].astype(jnp.bfloat16), 'dp', axis=...]
    dynamic_update_slice x0 -> x32, local copies, waits for them, and re-layouts: none -> 23.1 us  [the longest x16 11.5 us: order_regions(): lax.dynamic_update_slice_in_dim(res, a_now, (tile_out - j) % x_now * vec_...]
  transfers between devices with their start and end apart: 34 -> 64, of which waited for: 26 -> 41; matrix products, arithmetic and copies ran while one was open for 15% -> 17% of each run, Pallas kernels for 0% -> 0%
where the time goes in v1:
time: 2260 us; the launch traced here: 2250 us
  waiting for transfers between devices  1410 us (62%)
  matrix products  282 us (12%)
  blocking collectives  216 us (10%)
  local copies, waits for them, and re-layouts  177 us (8%)
  other arithmetic  82.6 us (4%)
  starting transfers between devices  65.8 us (3%)
    unnamed x38, waiting for transfers between devices  465 us
    reduce_scatter x8, waiting for transfers between devices, reduce_rows(): lax.psum_scatter(term_fn(jnp.int32(0), row_count * lax.axis_size('tensor'...  209 us
    reduce_scatter x2, waiting for transfers between devices, on_device(): lax.psum_scatter(grad_up.astype(jnp.bfloat16), 'dp', scatter_dimension=0,...  149 us
    reduce_scatter x2, waiting for transfers between devices, on_device(): lax.psum_scatter(grad_down.astype(jnp.bfloat16), 'dp', scatter_dimension=...  147 us
    all_gather x8, waiting for transfers between devices, collect(): return lax.all_gather(local_rows, 'tensor', axis=0, tiled=True)  132 us
    reduce_scatter x2, waiting for transfers between devices, on_device(): lax.psum_scatter(grad_out.astype(jnp.bfloat16), 'dp', scatter_dimension=1...  116 us
    all_gather x2, waiting for transfers between devices, on_device(): lax.all_gather(up_weight[layer_index].astype(jnp.bfloat16), 'dp', axis=0,...  81.7 us
    all_gather x1, blocking collectives, on_device(): lax.all_gather(row_biases, ('dp', 'tensor'), axis=2, tiled=True)  79 us
  transfers between devices with their start and end apart: 64, of which 41 were waited for; matrix products, arithmetic and copies ran while one was open for 17% of the time, Pallas kernels for 0%

profile of v1, /device:TPU:0, one launch (start us, length us, event | category | flops | bytes accessed | tf_op | source)
XLA Modules:
  0.0 2253.1 jit_solution(18301795725794424769)
XLA Ops:
  12.5 79.0 %all_gather.65 = f32[2,6,1024]{1,0,2:T(2,128)S(1)} all-gather(f32[2,6,32]{1,0,2:T(2,128)S(1)} %copy.99), channel_id=1, replica_groups=mesh['dp'=16,'tensor'=2] {'dp','tensor'}, dimensions={2}, use_global_device_ids=true | all-gather | bytes 50688 | tf_op jit(solution)/shard_map/all_gather | solution.py:152
  91.5 27.5 %fusion.137 = (f32[1,1,1024]{1,0,2:T(1,128)S(1)}, f32[1,1,1024]{1,0,2:T(1,128)S(1)}, f32[1,1,1024]{1,0,2:T(1,128)S(1)}, f32[1024]{0:T(1024)S(1)}, f32[1024]{0:T(...) fusion(f32[2,6,1024]{1,0,2:T(2,128)S(1)} %all_gather.65), kind=kLoop, calls=%fused_computation.320 | loop fusion | bytes 98304 | tf_op jit(solution)/shard_map/slice | solution.py:173
  123.9 5.9 add_convert_fusion.1
  134.7 17.3 while.44
  156.5 71.3 %all_gather.67 = f32[2,2,1024]{1,0,2:T(2,128)S(1)} all-gather(f32[2,2,32]{1,0,2:T(2,128)S(1)} %copy.104), channel_id=1, replica_groups=mesh['dp'=16,'tensor'=2] {'dp','tensor'}, dimensions={2}, use_global_device_ids=true | all-gather | bytes 16896 | tf_op jit(solution)/shard_map/all_gather | solution.py:151
  227.8 26.7 %slice_reduce_fusion.1 = (f32[1024]{0:T(1024)}, f32[1024]{0:T(1024)}, f32[1024]{0:T(1024)S(1)}, f32[1024]{0:T(1024)S(1)}) fusion(f32[2,2,1024]{1,0,2:T(2,128)S(1)} %all_gather.67), kind=kLoop, calls=%fused_computation.218 | loop fusion | bytes 32768 | tf_op jit(solution)/shard_map/slice | solution.py:195
  268.8 65.8 %all_gather.69 = f32[2,4096]{1,0:T(2,128)S(1)} all-gather(f32[2,128]{1,0:T(2,128)S(1)} %copy-done.80), channel_id=1, replica_groups=mesh['dp'=16,'tensor'=2] {'dp','tensor'}, dimensions={1}, use_global_device_ids=true | all-gather | bytes 33792 | tf_op jit(solution)/shard_map/all_gather | solution.py:153
  392.8 7.0 collective-permute-done.14
  400.6 25.7 %fusion.36 = (bf16[1024,2048]{1,0:T(8,128)(2,1)}, f32[1024,2048]{1,0:T(8,128)}) fusion(f32[2048]{0:T(1024)S(1)} %bitcast.432, bf16[1024,1024]{1,0:T(8,128)(2,1)} %all-gather.27.cloned.1.call-done, bf16[1024,2048]{1,0:T(8,128)(2,1)} %constant_dynamic-update-slice_fusion.24), kind=kOutput, calls=%fused_computation.80 | convolution fusion | flops 4433379328 | bytes 18882560 | tf_op jit(solution)/shard_map/dot_general | solution.py:191
  426.3 9.3 fusion.100
  436.5 27.1 %reduce-scatter.26.cloned.1.call-done = bf16[512,1024]{1,0:T(8,128)(2,1)} async-done(((bf16[1024,1024]{1,0:T(8,128)(2,1)}), bf16[512,1024]{1,0:T(8,128)(2,1)}) %reduce-scatter.26.cloned.1.call-update) | async-done | bytes 1048592 | tf_op jit(solution)/shard_map/reduce_scatter | solution.py:62
  469.5 41.4 %all-gather.47.cloned.1.call-done = bf16[1,3,1024,512]{3,2,1,0:T(8,128)(2,1)} async-done(((bf16[1,3,64,512]{3,2,1,0:T(8,128)(2,1)}), bf16[1,3,1024,512]{3,2,1,0:T(8,128)(2,1)}) %all-gather.47.cloned.1.call-update) | async-done | bytes 3145744 | tf_op jit(solution)/shard_map/all_gather | solution.py:167
  511.0 34.1 %all-gather.29.cloned.1.call-done = bf16[1024,1024]{1,0:T(8,128)(2,1)} async-done(((bf16[512,1024]{1,0:T(8,128)(2,1)}), bf16[1024,1024]{1,0:T(8,128)(2,1)}) %all-gather.29.cloned.1.call-update) | async-done | bytes 2097168 | tf_op jit(solution)/shard_map/all_gather | solution.py:58
  545.1 5.9 add_convert_fusion
  555.5 17.3 while.45
  572.8 12.3 all-gather.49.cloned.1.call-done
  589.0 30.8 %reduce-scatter.28.cloned.1.call-done = bf16[512,1024]{1,0:T(8,128)(2,1)} async-done(((bf16[1024,1024]{1,0:T(8,128)(2,1)}), bf16[512,1024]{1,0:T(8,128)(2,1)}) %reduce-scatter.28.cloned.1.call-update) | async-done | bytes 1048592 | tf_op jit(solution)/shard_map/reduce_scatter | solution.py:62
  674.1 7.7 collective-permute-done.25
  692.5 11.5 collective-permute-done.29
  704.7 25.6 %fusion.39 = (bf16[1024,2048]{1,0:T(8,128)(2,1)}, f32[1024,2048]{1,0:T(8,128)}) fusion(f32[2048]{0:T(1024)S(1)} %bitcast.435, bf16[1024,1024]{1,0:T(8,128)(2,1)} %all-gather.31.cloned.1.call-done, bf16[1024,2048]{1,0:T(8,128)(2,1)} %constant_dynamic-update-slice_fusion.8), kind=kOutput, calls=%fused_computation.83 | convolution fusion | flops 4433379328 | bytes 18882560 | tf_op jit(solution)/shard_map/dot_general | solution.py:191
  730.3 9.3 fusion.103
  739.9 27.6 %reduce-scatter.30.cloned.1.call-done = bf16[512,1024]{1,0:T(8,128)(2,1)} async-done(((bf16[1024,1024]{1,0:T(8,128)(2,1)}), bf16[512,1024]{1,0:T(8,128)(2,1)}) %reduce-scatter.30.cloned.1.call-update) | async-done | bytes 1048592 | tf_op jit(solution)/shard_map/reduce_scatter | solution.py:62
  776.4 32.7 %all-gather.33.cloned.1.call-done = bf16[1024,1024]{1,0:T(8,128)(2,1)} async-done(((bf16[512,1024]{1,0:T(8,128)(2,1)}), bf16[1024,1024]{1,0:T(8,128)(2,1)}) %all-gather.33.cloned.1.call-update) | async-done | bytes 2097168 | tf_op jit(solution)/shard_map/all_gather | solution.py:58
  809.0 12.5 convert_reduce_fusion
  821.5 40.1 %all-gather.53.cloned.1.call-done = bf16[1,1024,2048]{2,1,0:T(8,128)(2,1)} async-done(((bf16[1,64,2048]{2,1,0:T(8,128)(2,1)}), bf16[1,1024,2048]{2,1,0:T(8,128)(2,1)}) %all-gather.53.cloned.1.call-update) | async-done | bytes 4194320 | tf_op jit(solution)/shard_map/all_gather | solution.py:235
  861.6 9.3 fusion.106
  871.0 30.4 %reduce-scatter.32.cloned.1.call-done = bf16[512,1024]{1,0:T(8,128)(2,1)} async-done(((bf16[1024,1024]{1,0:T(8,128)(2,1)}), bf16[512,1024]{1,0:T(8,128)(2,1)}) %reduce-scatter.32.cloned.1.call-update) | async-done | bytes 1048592 | tf_op jit(solution)/shard_map/reduce_scatter | solution.py:62
  909.1 32.8 %all-gather.35.cloned.1.call-done = bf16[1024,1024]{1,0:T(8,128)(2,1)} async-done(((bf16[512,1024]{1,0:T(8,128)(2,1)}), bf16[1024,1024]{1,0:T(8,128)(2,1)}) %all-gather.35.cloned.1.call-update) | async-done | bytes 2097168 | tf_op jit(solution)/shard_map/all_gather | solution.py:58
  947.6 43.5 %while.46 = (s32[]{:T(128)}, bf16[2,512,3,512]{1,3,2,0:T(8,128)(2,1)}, bf16[2,512,512]{1,2,0:T(8,128)(2,1)}, s32[2,512]{1,0:T(2,128)S(1)}, bf16[2,512,512]{1,2,0...) while((s32[]{:T(128)}, ...), condition=%wide.region_27.28_spmd, body=%wide.region_25.27_spmd.sunk | while | flops 1379921920 | bytes 107076288 | solution.py:264
  950.0 4.5 fusion.261
  955.1 5.1 multiply_reduce_fusion.16
  976.8 5.1 multiply_reduce_fusion.16
  991.1 4.7 copy.110
  995.8 7.7 bitcast_convert_fusion.1
  1003.8 31.8 %reduce-scatter.34.cloned.1.call-done = bf16[512,1024]{1,0:T(8,128)(2,1)} async-done(((bf16[1024,1024]{1,0:T(8,128)(2,1)}), bf16[512,1024]{1,0:T(8,128)(2,1)}) %reduce-scatter.34.cloned.1.call-update) | async-done | bytes 1048592 | tf_op jit(solution)/shard_map/reduce_scatter | solution.py:62
  1043.6 32.5 %all-gather.37.cloned.1.call-done = bf16[1024,1024]{1,0:T(8,128)(2,1)} async-done(((bf16[512,1024]{1,0:T(8,128)(2,1)}), bf16[1024,1024]{1,0:T(8,128)(2,1)}) %all-gather.37.cloned.1.call-update) | async-done | bytes 2097168 | tf_op jit(solution)/shard_map/all_gather | solution.py:58
  1076.1 11.9 convert_reduce_fusion.1
  1088.0 41.5 %all-gather.55.cloned.1.call-done = bf16[1,1024,2048]{2,1,0:T(8,128)(2,1)} async-done(((bf16[1,64,2048]{2,1,0:T(8,128)(2,1)}), bf16[1,1024,2048]{2,1,0:T(8,128)(2,1)}) %all-gather.55.cloned.1.call-update) | async-done | bytes 4194320 | tf_op jit(solution)/shard_map/all_gather | solution.py:235
  1129.6 9.4 fusion.109
  1139.1 30.4 %reduce-scatter.36.cloned.1.call-done = bf16[512,1024]{1,0:T(8,128)(2,1)} async-done(((bf16[1024,1024]{1,0:T(8,128)(2,1)}), bf16[512,1024]{1,0:T(8,128)(2,1)}) %reduce-scatter.36.cloned.1.call-update) | async-done | bytes 1048592 | tf_op jit(solution)/shard_map/reduce_scatter | solution.py:62
  1182.8 10.1 convolution_convert_fusion
  1194.4 8.3 convolution_convert_fusion.1
  1204.3 8.3 convolution_convert_fusion.2
  1215.4 8.3 convolution_convert_fusion.3
  1230.8 43.6 %while.47 = (s32[]{:T(128)}, bf16[2,512,3,512]{1,3,2,0:T(8,128)(2,1)}, bf16[2,512,512]{1,2,0:T(8,128)(2,1)}, s32[2,512]{1,0:T(2,128)S(1)}, bf16[2,512,512]{1,2,0...) while((s32[]{:T(128)}, ...), condition=%wide.region_36.37_spmd, body=%wide.region_34.36_spmd.sunk | while | flops 1379921920 | bytes 107076288 | solution.py:264
  1238.2 5.1 multiply_reduce_fusion.17
  1260.1 5.1 multiply_reduce_fusion.17
  1287.3 6.0 convert_bitcast_fusion
  1293.3 5.7 copy.116
  1299.0 4.7 copy.112
  1303.7 6.0 convert_bitcast_fusion.1
  1309.7 5.8 copy.114
  1317.4 6.5 bitcast_convert_fusion
  1325.3 25.3 %reduce-scatter.56.cloned.1.call-done = f32[128,2]{1,0:T(8,128)} async-done(((f32[4096,2]{1,0:T(8,128)}), f32[128,2]{1,0:T(8,128)}) %reduce-scatter.56.cloned.1.call-update) | async-done | bytes 1040
  1352.1 131.6 %reduce-scatter.52.cloned.1.call-done = f32[32,4]{1,0:T(8,128)} async-done(((f32[1024,4]{1,0:T(8,128)}), f32[32,4]{1,0:T(8,128)}) %reduce-scatter.52.cloned.1.call-update) | async-done | bytes 528
  1485.2 71.4 %reduce-scatter.50.cloned.1.call-done = bf16[2048,64]{0,1:T(8,128)(2,1)} async-done(((bf16[2048,1024]{0,1:T(8,128)(2,1)}), bf16[2048,64]{0,1:T(8,128)(2,1)}) %reduce-scatter.50.cloned.1.call-update) | async-done | bytes 262160 | tf_op jit(solution)/shard_map/reduce_scatter | solution.py:320
  1556.5 75.5 %reduce-scatter.48.cloned.1.call-done = bf16[2048,64]{0,1:T(8,128)(2,1)} async-done(((bf16[2048,1024]{0,1:T(8,128)(2,1)}), bf16[2048,64]{0,1:T(8,128)(2,1)}) %reduce-scatter.48.cloned.1.call-update) | async-done | bytes 262160 | tf_op jit(solution)/shard_map/reduce_scatter | solution.py:320
  1634.0 73.8 %reduce-scatter.46.cloned.1.call-done = bf16[64,2048]{1,0:T(8,128)(2,1)} async-done(((bf16[1024,2048]{1,0:T(8,128)(2,1)}), bf16[64,2048]{1,0:T(8,128)(2,1)}) %reduce-scatter.46.cloned.1.call-update) | async-done | bytes 262160 | tf_op jit(solution)/shard_map/reduce_scatter | solution.py:317
  1707.8 75.3 %reduce-scatter.44.cloned.1.call-done = bf16[64,2048]{1,0:T(8,128)(2,1)} async-done(((bf16[1024,2048]{1,0:T(8,128)(2,1)}), bf16[64,2048]{1,0:T(8,128)(2,1)}) %reduce-scatter.44.cloned.1.call-update) | async-done | bytes 262160 | tf_op jit(solution)/shard_map/reduce_scatter | solution.py:317
  1785.2 133.0 %reduce-scatter.54.cloned.1.call-done = f32[32,12]{1,0:T(8,128)} async-done(((f32[1024,12]{1,0:T(8,128)}), f32[32,12]{1,0:T(8,128)}) %reduce-scatter.54.cloned.1.call-update) | async-done | bytes 1552
  1919.6 55.4 %reduce-scatter.42.cloned.1.call-done = bf16[512,64]{0,1:T(8,128)(2,1)} async-done(((bf16[512,1024]{0,1:T(8,128)(2,1)}), bf16[512,64]{0,1:T(8,128)(2,1)}) %reduce-scatter.42.cloned.1.call-update) | async-done | bytes 65552 | tf_op jit(solution)/shard_map/reduce_scatter | solution.py:314
  1975.1 60.5 %reduce-scatter.40.cloned.1.call-done = bf16[512,64]{0,1:T(8,128)(2,1)} async-done(((bf16[512,1024]{0,1:T(8,128)(2,1)}), bf16[512,64]{0,1:T(8,128)(2,1)}) %reduce-scatter.40.cloned.1.call-update) | async-done | bytes 65552 | tf_op jit(solution)/shard_map/reduce_scatter | solution.py:314
  2037.2 171.4 %all-reduce.5.cloned.1.call-done = (bf16[3,1024,512]{2,0,1:T(4,128)(2,1)}, bf16[3,1024,512]{2,0,1:T(4,128)(2,1)}) async-done(((bf16[3,1024,512]{2,0,1:T(4,128)(2,1)}, bf16[3,1024,512]{2,0,1:T(4,128)(2,1)}), (bf16[3,1024,512]{2,0,1:T(4,128)(2,1)}, bf16[3,1024,512]{2,0,1:T(4,128)(2,1)})) %all-reduce.5.cloned.1.call-update) | async-done | bytes 6291472
  2212.1 31.1 %reduce-scatter.38.cloned.1.call-done = bf16[512,1024]{1,0:T(8,128)(2,1)} async-done(((bf16[1024,1024]{1,0:T(8,128)(2,1)}), bf16[512,1024]{1,0:T(8,128)(2,1)}) %reduce-scatter.38.cloned.1.call-update) | async-done | bytes 1048592 | tf_op jit(solution)/shard_map/reduce_scatter | solution.py:62
  (573 shorter events, 357.3 us)
Async XLA Ops:
  7.2 116.7 %all-gather.25.cloned.1.call-start = ((), (), s32[]{:S(2)}) async-start(), calls=%async_computation.17 | async-start | bytes 3145728 | tf_op jit(solution)/shard_map/all_gather | solution.py:58
  7.9 116.0 %all-gather.41.cloned.1.call-start = ((), (), s32[]{:S(2)}) async-start(), calls=%async_computation.39 | async-start | bytes 3342336 | tf_op jit(solution)/shard_map/all_gather | solution.py:167
  9.9 142.2 %all-gather.43.cloned.1.call-start = ((), (), s32[]{:S(2)}) async-start(), calls=%async_computation.40 | async-start | bytes 1114112 | tf_op jit(solution)/shard_map/all_gather | solution.py:168
  11.6 242.8 %reduce-scatter.24.cloned.1.call-start = ((), (), s32[]{:S(2)}) async-start(), calls=%async_computation.18 | async-start | bytes 3145728 | tf_op jit(solution)/shard_map/reduce_scatter | solution.py:62
  156.3 244.2 %all-gather.27.cloned.1.call-start = ((), (), s32[]{:S(2)}) async-start(), calls=%async_computation.19 | async-start | bytes 3145728 | tf_op jit(solution)/shard_map/all_gather | solution.py:58
  259.6 166.7 %all-gather.45.cloned.1.call-start = ((), (), s32[]{:S(2)}) async-start(), calls=%async_computation.41 | async-start | bytes 4456448 | tf_op jit(solution)/shard_map/all_gather | solution.py:170
  262.0 76.5 %collective-permute-start = (bf16[64,2048]{1,0:T(8,128)(2,1)S(1)}, bf16[64,2048]{1,0:T(8,128)(2,1)S(1)}, u32[]{:S(2)}, u32[]{:S(2)}) collective-permute-start(bf16[64,2048]{1,0:T(8,128)(2,1)S(1)} %get-tuple-element.416), channel_id=1, source_target_pairs={{0,2},{2,4},{4,6},{6,8},{8,10},{10,12},{12,14},{14,16},{16,18},{18... | collective-permute-start | bytes 786440 | tf_op jit(solution)/shard_map/ppermute | solution.py:31
  262.0 76.5 %collective-permute-start.1 = (bf16[64,2048]{1,0:T(8,128)(2,1)S(1)}, bf16[64,2048]{1,0:T(8,128)(2,1)S(1)}, u32[]{:S(2)}, u32[]{:S(2)}) collective-permute-start(bf16[64,2048]{1,0:T(8,128)(2,1)S(1)} %get-tuple-element.416), channel_id=1, source_target_pairs={{0,30},{2,0},{4,2},{6,4},{8,6},{10,8},{12,10},{14,12},{16,14},{18,... | collective-permute-start | bytes 786440 | tf_op jit(solution)/shard_map/ppermute | solution.py:36
  268.7 194.8 %reduce-scatter.26.cloned.1.call-start = ((), (), s32[]{:S(2)}) async-start(), calls=%async_computation.20 | async-start | bytes 3145728 | tf_op jit(solution)/shard_map/reduce_scatter | solution.py:62
  338.6 9.9 collective-permute-start.2
  338.6 9.9 collective-permute-start.3
  348.5 8.6 collective-permute-start.4
  348.5 8.6 collective-permute-start.5
  357.1 8.6 collective-permute-start.6
  357.1 8.6 collective-permute-start.7
  365.7 8.6 collective-permute-start.8
  365.7 8.6 collective-permute-start.9
  374.3 8.6 collective-permute-start.10
  374.3 8.6 collective-permute-start.11
  382.9 8.5 collective-permute-start.12
  382.9 9.2 collective-permute-start.13
  391.4 8.5 collective-permute-start.14
  435.7 75.3 %all-gather.47.cloned.1.call-start = ((), (), s32[]{:S(2)}) async-start(), calls=%async_computation.42 | async-start | bytes 3342336 | tf_op jit(solution)/shard_map/all_gather | solution.py:167
  436.4 108.6 %all-gather.29.cloned.1.call-start = ((), (), s32[]{:S(2)}) async-start(), calls=%async_computation.21 | async-start | bytes 3145728 | tf_op jit(solution)/shard_map/all_gather | solution.py:58
  468.5 116.6 %all-gather.49.cloned.1.call-start = ((), (), s32[]{:S(2)}) async-start(), calls=%async_computation.43 | async-start | bytes 1114112 | tf_op jit(solution)/shard_map/all_gather | solution.py:168
  469.1 150.8 %reduce-scatter.28.cloned.1.call-start = ((), (), s32[]{:S(2)}) async-start(), calls=%async_computation.22 | async-start | bytes 3145728 | tf_op jit(solution)/shard_map/reduce_scatter | solution.py:62
  589.0 115.8 %all-gather.31.cloned.1.call-start = ((), (), s32[]{:S(2)}) async-start(), calls=%async_computation.23 | async-start | bytes 3145728 | tf_op jit(solution)/shard_map/all_gather | solution.py:58
  624.9 105.4 %all-gather.51.cloned.1.call-start = ((), (), s32[]{:S(2)}) async-start(), calls=%async_computation.44 | async-start | bytes 4456448 | tf_op jit(solution)/shard_map/all_gather | solution.py:170
  625.0 8.7 collective-permute-start.15
  625.0 9.3 collective-permute-start.16
  629.5 138.0 %reduce-scatter.30.cloned.1.call-start = ((), (), s32[]{:S(2)}) async-start(), calls=%async_computation.24 | async-start | bytes 3145728 | tf_op jit(solution)/shard_map/reduce_scatter | solution.py:62
  633.6 8.6 collective-permute-start.17
  634.3 8.6 collective-permute-start.18
  642.2 8.6 collective-permute-start.19
  642.9 8.8 collective-permute-start.20
  650.8 8.8 collective-permute-start.21
  651.8 8.6 collective-permute-start.22
  659.6 8.6 collective-permute-start.23
  660.4 8.6 collective-permute-start.24
  668.2 13.6 collective-permute-start.25
  669.0 13.6 collective-permute-start.26
  681.8 8.5 collective-permute-start.27
  682.5 9.3 collective-permute-start.28
  690.3 13.7 collective-permute-start.29
  739.6 69.4 %all-gather.33.cloned.1.call-start = ((), (), s32[]{:S(2)}) async-start(), calls=%async_computation.25 | async-start | bytes 3145728 | tf_op jit(solution)/shard_map/all_gather | solution.py:58
  775.7 85.9 %all-gather.53.cloned.1.call-start = ((), (), s32[]{:S(2)}) async-start(), calls=%async_computation.45 | async-start | bytes 4456448 | tf_op jit(solution)/shard_map/all_gather | solution.py:235
  776.3 125.1 %reduce-scatter.32.cloned.1.call-start = ((), (), s32[]{:S(2)}) async-start(), calls=%async_computation.26 | async-start | bytes 3145728 | tf_op jit(solution)/shard_map/reduce_scatter | solution.py:62
  871.0 70.9 %all-gather.35.cloned.1.call-start = ((), (), s32[]{:S(2)}) async-start(), calls=%async_computation.27 | async-start | bytes 3145728 | tf_op jit(solution)/shard_map/all_gather | solution.py:58
  908.6 127.0 %reduce-scatter.34.cloned.1.call-start = ((), (), s32[]{:S(2)}) async-start(), calls=%async_computation.28 | async-start | bytes 3145728 | tf_op jit(solution)/shard_map/reduce_scatter | solution.py:62
  1003.6 72.5 %all-gather.37.cloned.1.call-start = ((), (), s32[]{:S(2)}) async-start(), calls=%async_computation.29 | async-start | bytes 3145728 | tf_op jit(solution)/shard_map/all_gather | solution.py:58
  1042.8 86.8 %all-gather.55.cloned.1.call-start = ((), (), s32[]{:S(2)}) async-start(), calls=%async_computation.46 | async-start | bytes 4456448 | tf_op jit(solution)/shard_map/all_gather | solution.py:235
  1043.5 126.0 %reduce-scatter.36.cloned.1.call-start = ((), (), s32[]{:S(2)}) async-start(), calls=%async_computation.30 | async-start | bytes 3145728 | tf_op jit(solution)/shard_map/reduce_scatter | solution.py:62
  1139.1 84.9 %all-gather.39.cloned.1.call-start = ((), (), s32[]{:S(2)}) async-start(), calls=%async_computation.31 | async-start | bytes 3145728 | tf_op jit(solution)/shard_map/all_gather | solution.py:58
  1178.0 172.6 %reduce-scatter.56.cloned.1.call-start = ((), (), s32[]{:S(2)}) async-start(), calls=%async_computation.49 | async-start | bytes 2162688
  1180.6 303.1 %reduce-scatter.52.cloned.1.call-start = ((), (), s32[]{:S(2)}) async-start(), calls=%async_computation.47 | async-start | bytes 540672
  1182.7 373.8 %reduce-scatter.50.cloned.1.call-start = ((), (), s32[]{:S(2)}) async-start(), calls=%async_computation.38 | async-start | bytes 4456448 | tf_op jit(solution)/shard_map/reduce_scatter | solution.py:320
  1192.8 439.1 %reduce-scatter.48.cloned.1.call-start = ((), (), s32[]{:S(2)}) async-start(), calls=%async_computation.37 | async-start | bytes 4456448 | tf_op jit(solution)/shard_map/reduce_scatter | solution.py:320
  1202.7 505.1 %reduce-scatter.46.cloned.1.call-start = ((), (), s32[]{:S(2)}) async-start(), calls=%async_computation.36 | async-start | bytes 4456448 | tf_op jit(solution)/shard_map/reduce_scatter | solution.py:317
  1212.7 570.4 %reduce-scatter.44.cloned.1.call-start = ((), (), s32[]{:S(2)}) async-start(), calls=%async_computation.35 | async-start | bytes 4456448 | tf_op jit(solution)/shard_map/reduce_scatter | solution.py:317
  1223.7 694.5 %reduce-scatter.54.cloned.1.call-start = ((), (), s32[]{:S(2)}) async-start(), calls=%async_computation.48 | async-start | bytes 540672
  1279.0 696.0 %reduce-scatter.42.cloned.1.call-start = ((), (), s32[]{:S(2)}) async-start(), calls=%async_computation.34 | async-start | bytes 1114112 | tf_op jit(solution)/shard_map/reduce_scatter | solution.py:314
  1283.0 752.5 %reduce-scatter.40.cloned.1.call-start = ((), (), s32[]{:S(2)}) async-start(), calls=%async_computation.33 | async-start | bytes 1114112 | tf_op jit(solution)/shard_map/reduce_scatter | solution.py:314
  1287.2 921.3 %all-reduce.5.cloned.1.call-start = ((), (), s32[]{:S(2)}) async-start(), calls=%async_computation.50 | async-start | bytes 16777216
  1315.6 927.6 %reduce-scatter.38.cloned.1.call-start = ((), (), s32[]{:S(2)}) async-start(), calls=%async_computation.32 | async-start | bytes 3145728 | tf_op jit(solution)/shard_map/reduce_scatter | solution.py:62
  (97 other events, 5248.6 us)
Sparse Core Ops, SparseCore 0:
  9.6 44.2 all-gather.24
  56.6 47.2 all-gather.40
  106.6 36.7 all-gather.42
  156.5 37.5 reduce-scatter.23
  259.8 31.2 all-gather.26
  293.9 59.0 all-gather.44
  435.8 27.7 reduce-scatter.25
  465.7 45.2 all-gather.46
  513.1 31.9 all-gather.28
  547.1 37.9 all-gather.48
  589.1 30.7 reduce-scatter.27
  625.0 33.0 all-gather.30
  660.6 53.7 all-gather.50
  739.7 27.6 reduce-scatter.29
  775.8 33.1 all-gather.32
  811.0 50.5 all-gather.52
  871.1 30.3 reduce-scatter.31
  908.7 33.0 all-gather.34
  1003.7 31.8 reduce-scatter.33
  1042.9 33.1 all-gather.36
  1078.8 50.7 all-gather.54
  1139.2 30.3 reduce-scatter.35
  1178.1 33.1 all-gather.38
  1213.5 137.0 reduce-scatter.55
  1353.4 130.2 reduce-scatter.51
  1487.9 68.5 reduce-scatter.49
  1560.2 71.7 reduce-scatter.47
  1636.3 71.4 reduce-scatter.45
  1711.7 71.3 reduce-scatter.43
  1785.3 132.8 reduce-scatter.53
  1921.8 53.2 reduce-scatter.41
  1979.1 56.3 reduce-scatter.39
  2039.2 169.2 all-reduce.4
  2211.4 31.6 reduce-scatter.37
